TPU v7x, 32 devices: a whole 2x2x4 slice. The times are simulated.
32 devices in a mesh: row: 8 (over z, y), col: 4 (over x, core).
Axes of the slice: x: 2, y: 2, z: 4, core: 2. Of those that a mesh axis runs over, the one named last changes fastest.
Arguments:
- acts: bfloat16 [1024, 3072], P('row', 'col'), may hold values from -6 to 6
- grads: bfloat16 [1024, 3072], P('col', 'row'), may hold values from -0.19921875 to 0.19921875
- next_acts: bfloat16 [256, 3072], P('row', 'col'), may hold values from -6 to 6
- weight: bfloat16 [3072, 3072], P('row', 'col'), may hold values from -0.109375 to 0.109375
- moment: float32 [3072, 3072], P('row', 'col'), may hold values from -6 to 6
- second: float32 [3072, 3072], P('row', 'col'), may hold values from 0.05 to 5
- left_bank: bfloat16 [4, 384, 384], replicated, may hold values from -1 to 1, as said below
- right_bank: bfloat16 [4, 768, 768], P(None, 'row'), may hold values from -1 to 1, as said below
- left_index: int32 [8, 4], P('row', 'col'), may hold values from 0 to 3
- right_index: int32 [8, 4], P('row', 'col'), may hold values from 0 to 3
Outputs:
- update: bfloat16 [3072, 3072], P('row', 'col')
- next_out: bfloat16 [256, 3072], P('col', 'row')
Inputs may be any that keep to these rules, and one draw needn't show every extreme that they name: `left_bank`: each basis is an orthogonal matrix rounded to bfloat16. `right_bank`: each basis is an orthogonal matrix rounded to bfloat16.
All inputs are finite; a program needn't handle non-finite values.
Results may differ from a plain program's by a relative error of at most 0.008.
Values may be sent and summed in bfloat16 or wider, within the bound.
A program may use at most 64 MiB of HBM per device.

v0:
```python
import jax
import jax.numpy as jnp
from jax import lax
from jax.sharding import PartitionSpec as P


def per_device(
    acts, grads, next_acts, weight, moment, second, left_bank, right_bank, left_index, right_index
):
    f32 = jnp.float32
    full_acts = lax.all_gather(acts, "row", axis=0, tiled=True)
    full_grads = lax.all_gather(grads, "col", axis=0, tiled=True)
    gradient = lax.dot_general(
        full_grads, full_acts, (((0,), (0,)), ((), ())), preferred_element_type=f32
    ).astype(jnp.bfloat16)
    left_basis = lax.dynamic_index_in_dim(left_bank, left_index[0, 0], 0, keepdims=False)
    half = lax.dot_general(
        left_basis, gradient, (((0,), (0,)), ((), ())), preferred_element_type=f32
    ).astype(jnp.bfloat16)
    all_picks = lax.all_gather(right_index[:, 0], "row", axis=0, tiled=True)
    outgoing = jnp.take(right_bank, all_picks, axis=0)
    incoming = lax.all_to_all(outgoing, "row", split_axis=0, concat_axis=0, tiled=True)
    right_basis = incoming.reshape(right_bank.shape[2], right_bank.shape[2])
    rotated = jnp.dot(half, right_basis, preferred_element_type=f32)
    new_moment = 0.8 * moment + 0.2 * rotated
    new_second = 0.9 * second + 0.1 * rotated * rotated
    scaled = (new_moment / (jnp.sqrt(new_second) + 1e-08)).astype(jnp.bfloat16)
    back_left = jnp.dot(left_basis, scaled, preferred_element_type=f32).astype(jnp.bfloat16)
    update_full = lax.dot_general(
        back_left, right_basis, (((1,), (1,)), ((), ())), preferred_element_type=f32
    )
    new_weight = (weight.astype(f32) - 0.001 * update_full).astype(jnp.bfloat16)
    full_next = lax.all_gather(next_acts, "row", axis=0, tiled=True)
    summed = lax.psum_scatter(
        lax.dot_general(
            full_next, new_weight, (((1,), (1,)), ((), ())), preferred_element_type=f32
        ),
        "col",
        scatter_dimension=0,
        tiled=True,
    )
    return (update_full.astype(jnp.bfloat16), summed.astype(jnp.bfloat16))


def solution(mesh):
    return jax.shard_map(
        per_device,
        mesh=mesh,
        in_specs=(
            P("row", "col"),
            P("col", "row"),
            P("row", "col"),
            P("row", "col"),
            P("row", "col"),
            P("row", "col"),
            P(),
            P(None, "row", None),
            P("row", "col"),
            P("row", "col"),
        ),
        out_specs=(P("row", "col"), P("col", "row")),
        check_vma=False,
    )
```

profile of v0, /device:TPU:0, one launch (start us, length us, event | category | flops | bytes accessed | tf_op | source)
XLA Modules:
  0.0 140.9 jit_solution(1534961277164715009)
XLA Ops:
  7.2 0.0 copy-start
  7.2 0.0 all-gather.3.cloned.1.call-start
  7.2 0.7 all-gather.3.cloned.1.call-update
  8.6 1.2 dynamic-slice
  9.8 0.7 bitcast_dynamic-update-slice_fusion
  10.5 13.1 %all-reduce = s32[8]{0:T(128)S(1)} all-reduce(s32[8]{0:T(128)S(1)} %bitcast_dynamic-update-slice_fusion), channel_id=2, replica_groups=mesh['row'=8,'col'=4] {'row'}, use_global_device_ids=true, to_apply=%add | all-reduce | flops 8 | bytes 64 | tf_op jit(solution)/shard_map/all_gather | solution.py:20
  23.6 1.7 %gather_fusion = bf16[8,96,768]{2,1,0:T(8,128)(2,1)S(1)} fusion(bf16[4,96,768]{2,1,0:T(8,128)(2,1)} %param.17, s32[1024]{0:T(1024)S(1)} %pad_clamp_fusion), kind=kCustom, calls=%fused_computation | custom fusion | bytes 2359328 | tf_op jit(solution)/shard_map/jit(_take)/gather | solution.py:21
  25.3 1.2 broadcast_select_fusion
  26.5 0.0 copy-start.2
  26.5 3.7 %all-to-all-start = ((bf16[8,96,768]{2,1,0:T(8,128)(2,1)}), bf16[8,96,768]{2,1,0:T(8,128)(2,1)S(1)}, u32[]{:S(2)}, u32[]{:S(2)}) async-start(bf16[8,96,768]{2,1,0:T(8,128)(2,1)} %broadcast_select_fusion), calls=%async_computation | async-start | bytes 2359296 | tf_op jit(solution)/shard_map/all_to_all | solution.py:22
  30.2 0.0 reduce-scatter.4.cloned.1.call-start
  30.9 0.0 copy-done.2
  30.9 60.7 %all_gather.15 = bf16[256,768]{1,0:T(8,128)(2,1)S(1)} all-gather(bf16[32,768]{1,0:T(8,128)(2,1)S(1)} %copy-done.2), channel_id=1, replica_groups=mesh['row'=8,'col'=4] {'row'}, dimensions={0}, use_global_device_ids=true | all-gather | bytes 442368 | tf_op jit(solution)/shard_map/all_gather | solution.py:33
  91.6 8.8 %all_gather.12 = bf16[1024,384]{1,0:T(8,128)(2,1)S(1)} all-gather(bf16[256,384]{1,0:T(8,128)(2,1)} %param.11), channel_id=1, replica_groups=mesh['row'=8,'col'=4] {'col'}, dimensions={0}, use_global_device_ids=true | all-gather | bytes 983040 | tf_op jit(solution)/shard_map/all_gather | solution.py:12
  100.4 0.0 all-gather.3.cloned.1.call-done
  100.4 3.0 %convolution_convert_fusion.2 = bf16[384,768]{1,0:T(8,128)(2,1)} fusion(bf16[1024,384]{1,0:T(8,128)(2,1)S(1)} %all_gather.12, bf16[1024,768]{1,0:T(8,128)(2,1)} %all-gather.3.cloned.1.call-done), kind=kOutput, calls=%fused_computation.4 | convolution fusion | flops 604274688 | bytes 2949120 | tf_op jit(solution)/shard_map/dot_general | solution.py:13
  103.4 0.0 all-to-all-done
  103.4 0.0 copy-start.1
  103.4 1.0 copy-done.1
  104.5 0.0 copy-done
  104.5 3.3 %fusion.6 = bf16[384,768]{1,0:T(8,128)(2,1)S(1)} fusion(f32[384,768]{1,0:T(8,128)} %param.15, f32[384,768]{1,0:T(8,128)} %param.14, bf16[768,768]{1,0:T(8,128)(2,1)S(1)} %bitcast.27, bf16[384,768]{1,0:T(8,128)(2,1)} %convolution_convert_fusion.2, bf16[4,384,384]{2,1,0:T(8,128)(2,1)S(1)} %copy-done, s32[]{:T(128)S(6)} %select_n.13), kind=kOutput, calls=%fused_computation.13 | convolution fusion | flops 682721280 | bytes 5013508 | tf_op jit(solution)/shard_map/dot_general | solution.py:24
  107.8 3.2 %fusion.21 = (bf16[384,768]{1,0:T(8,128)(2,1)}, f32[384,768]{1,0:T(8,128)S(1)}) fusion(bf16[768,768]{1,0:T(8,128)(2,1)} %bitcast.28, bf16[384,768]{1,0:T(8,128)(2,1)S(1)} %fusion.6, bf16[4,384,384]{2,1,0:T(8,128)(2,1)S(1)} %copy-done, s32[]{:T(128)S(6)} %select_n.13), kind=kOutput, calls=%fused_computation.27 | convolution fusion | flops 680067072 | bytes 3833860 | tf_op jit(solution)/shard_map/dot_general | solution.py:29
  110.9 1.4 %convolution_bitcast_fusion = f32[256,384]{0,1:T(8,128)S(1)} fusion(bf16[256,768]{1,0:T(8,128)(2,1)S(1)} %all_gather.15, f32[384,768]{1,0:T(8,128)S(1)} %get-tuple-element.7, bf16[384,768]{1,0:T(8,128)(2,1)} %param.13), kind=kOutput, calls=%fused_computation.7 | convolution fusion | flops 152174592 | bytes 2555904 | tf_op jit(solution)/shard_map/dot_general | solution.py:35
  112.3 0.9 copy.14
  113.3 0.0 reduce-scatter.4.cloned.1.call-update
  113.3 19.1 %reduce-scatter.4.cloned.1.call-done = f32[64,384]{1,0:T(8,128)} async-done(((f32[256,384]{1,0:T(8,128)}), f32[64,384]{1,0:T(8,128)}) %reduce-scatter.4.cloned.1.call-update) | async-done | bytes 98320
  132.4 1.0 copy.15
  133.4 0.7 copy.13
  (4 shorter events, 0.0 us)
Async XLA Ops:
  7.2 97.3 %copy-start = (bf16[4,384,384]{2,1,0:T(8,128)(2,1)S(1)}, bf16[4,384,384]{2,1,0:T(8,128)(2,1)}, u32[]{:S(2)}) copy-start(bf16[4,384,384]{2,1,0:T(8,128)(2,1)} %param.16) | copy-start | bytes 3538948
  7.2 93.2 %all-gather.3.cloned.1.call-start = ((), (), s32[]{:S(2)}) async-start(), calls=%async_computation.2 | async-start | bytes 1769472 | tf_op jit(solution)/shard_map/all_gather | solution.py:11
  26.5 4.4 %copy-start.2 = (bf16[32,768]{1,0:T(8,128)(2,1)S(1)}, bf16[32,768]{1,0:T(8,128)(2,1)}, u32[]{:S(2)}) copy-start(bf16[32,768]{1,0:T(8,128)(2,1)} %param.12) | copy-start | bytes 147460
  26.5 76.9 %all-to-all-start = ((bf16[8,96,768]{2,1,0:T(8,128)(2,1)}), bf16[8,96,768]{2,1,0:T(8,128)(2,1)S(1)}, u32[]{:S(2)}, u32[]{:S(2)}) async-start(bf16[8,96,768]{2,1,0:T(8,128)(2,1)} %broadcast_select_fusion), calls=%async_computation | async-start | bytes 2359296 | tf_op jit(solution)/shard_map/all_to_all | solution.py:22
  30.2 102.2 %reduce-scatter.4.cloned.1.call-start = ((), (), s32[]{:S(2)}) async-start(), calls=%async_computation.3 | async-start | bytes 491520
  103.4 1.0 copy-start.1
Sparse Core Ops, SparseCore 0:
  10.2 60.5 all-gather.2
  113.4 18.9 reduce-scatter.3
where the time goes:
time: 141 us
  blocking collectives  82.6 us (59%)
  waiting for transfers between devices  19.8 us (14%)
  between operations  15.4 us (11%)
  matrix products  10.9 us (8%)
  local copies, waits for them, and re-layouts  7.28 us (5%)
  starting transfers between devices  3.77 us (3%)
    all_gather x1, blocking collectives, per_device(): full_next = lax.all_gather(next_acts, 'row', axis=0, tiled=True)  60.7 us
    unnamed x3, waiting for transfers between devices  19.8 us
    all_gather x1, blocking collectives, per_device(): all_picks = lax.all_gather(right_index[:, 0], 'row', axis=0, tiled=True)  13.1 us
    all_gather x1, blocking collectives, per_device(): full_grads = lax.all_gather(grads, 'col', axis=0, tiled=True)  8.79 us
    unnamed x12, local copies, waits for them, and re-layouts  5.6 us
    all_to_all x1, starting transfers between devices, per_device(): lax.all_to_all(outgoing, 'row', split_axis=0, concat_axis=0, tiled=True)  3.69 us
    dot_general x1, matrix products, per_device(): rotated = jnp.dot(half, right_basis, preferred_element_type=f32)  3.29 us
    dot_general x1, matrix products, per_device(): lax.dot_general(back_left, right_basis, (((1,), (1,)), ((), ())), preferr...  3.15 us
  transfers between devices with their start and end apart: 3, of which 1 were waited for; matrix products, arithmetic and copies ran while one was open for 6% of the time, Pallas kernels for 0%

commit v1 on v0

v1 whole, which is shorter than its diff:
```python
import functools

import jax
import jax.numpy as jnp
from jax import lax
from jax.experimental import pallas as pl
from jax.experimental.pallas import tpu as pltpu
from jax.sharding import PartitionSpec as P

F32 = jnp.float32
BF16 = jnp.bfloat16
MESH = pl.DeviceIdType.MESH


def flip(value, bits, size):
    out, place = 0, 1
    while place < size:
        bit = (value // place) % 2
        out = out + place * ((1 - bit) if (bits // place) % 2 else bit)
        place *= 2
    return out


def as_matrix(value):
    cols = value.shape[-1]
    if value.shape[-2] % 16:
        return value.astype(F32).reshape(-1, cols).astype(BF16)
    return value.reshape(-1, cols)


def kernel(
    nz, nc,
    acts, grads, nxt, weight, moment, second, left_bank, right_bank, left_index, right_index,
    update, out,
    afull, gfull, nfull, wbuf, mbuf, sbuf, lbuf, bz, sel, rbuf,
    my_pick, picks, picks_smem, gacc, half, back, part, rsend, rrecv, ubuf, obuf,
    local, a_s, a_r, ay_s, ay_r, n_s, n_r, ny_s, ny_r, b_s, b_r,
    g_s, g_r, p_s, p_r, s_s, s_r, r_s, r_r,
):
    row, col = lax.axis_index("row"), lax.axis_index("col")
    z, y = row // 2, row % 2
    quad, q = col // 4, col % 4
    x, k = q // 2, q % 2
    tok = acts.shape[0]
    gtok = grads.shape[0]
    width = acts.shape[1]
    lanes = width // 2
    slot = y * 4 + q
    my_lanes = pl.ds(pl.multiple_of(x * lanes, 128), lanes)

    def remote(src, dst, ss, rs, device):
        return pltpu.make_async_remote_copy(
            src_ref=src, dst_ref=dst, send_sem=ss, recv_sem=rs,
            device_id=device, device_id_type=MESH,
        )

    z_peers = [(d, flip(z, d, nz)) for d in range(1, nz)]
    plane = [
        (dy * 4 + dq, 2 * z + ((1 - y) if dy else y), quad * 4 + flip(q, dq, 4),
         ((1 - y) if dy else y) * 4 + flip(q, dq, 4))
        for dy in range(2) for dq in range(4) if dy or dq
    ]
    col_peers = [(d, flip(col, d, nc)) for d in range(1, nc)]
    far_cols = [peer for d, peer in col_peers if d >= 4]
    mate = (2 * z + 1 - y, col)

    my_pick[...] = jnp.full(my_pick.shape, right_index[0, 0], jnp.int32)

    loads = [
        (acts, afull.at[z, y]), (nxt, nfull.at[z, y]),
        (grads, gfull.at[pl.ds(pl.multiple_of(col * gtok, gtok), gtok)]),
        (weight, wbuf), (moment, mbuf), (second, sbuf), (left_bank, lbuf),
    ]
    loads = [pltpu.make_async_copy(s, d, local.at[i]) for i, (s, d) in enumerate(loads)]
    own_bank = pltpu.make_async_copy(
        right_bank.at[:, :, my_lanes], bz.at[z // 2], local.at[7]
    )

    @pl.when(z % 2 == k)
    def _():
        own_bank.start()

    for load in loads:
        load.start()

    barrier = pltpu.get_barrier_semaphore()
    friends = [(2 * p + y, col) for _, p in z_peers]
    friends += [(r, c) for _, r, c, _ in plane]
    friends += [(row, c) for c in far_cols]
    for friend in friends:
        pl.semaphore_signal(barrier, inc=1, device_id=friend, device_id_type=MESH)
    pl.semaphore_wait(barrier, len(friends))

    sends = []

    def go(copy):
        copy.start()
        sends.append(copy)

    for e, r, c, _ in plane:
        go(remote(my_pick, picks.at[slot], p_s.at[e], p_r.at[slot], (r, c)))
    bank_sends = [
        remote(right_bank.at[:, :, my_lanes], bz.at[z // 2], b_s.at[d], b_r.at[z // 2],
               (2 * p + y, col))
        for d, p in z_peers
    ]

    @pl.when(z % 2 == k)
    def _():
        for copy in bank_sends:
            copy.start()

    go(remote(acts, afull.at[z, y], ay_s.at[0], ay_r.at[z], mate))
    for d, p in z_peers:
        go(remote(acts, afull.at[z, y], a_s.at[d], a_r.at[z], (2 * p + y, col)))
    for d, c in col_peers:
        go(remote(grads, gfull.at[pl.ds(pl.multiple_of(col * gtok, gtok), gtok)],
                  g_s.at[d], g_r.at[col], (row, c)))
    for d, p in z_peers:
        go(remote(nxt, nfull.at[z, y], n_s.at[d], n_r.at[z], (2 * p + y, col)))

    picks[slot] = my_pick[...]
    for e, r, c, s in plane:
        remote(my_pick, picks.at[s], p_s.at[e], p_r.at[s], (r, c)).wait_recv()
    to_smem = pltpu.make_async_copy(picks, picks_smem, local.at[8])
    to_smem.start()
    to_smem.wait()

    for d in range(nz):
        zs = flip(z, d, nz) if d else z

        @pl.when(zs % 2 == k)
        def _(d=d, zs=zs):
            if d == 0:
                own_bank.wait()
            else:
                remote(right_bank.at[:, :, my_lanes], bz.at[zs // 2], b_s.at[d],
                       b_r.at[zs // 2], (2 * zs + y, col)).wait_recv()

    sel[0] = bz[:, picks_smem[slot, 0, 0]]
    for e, r, c, s in plane:
        sel[e] = bz[:, picks_smem[s, 0, 0]]
    own_sel = pltpu.make_async_copy(sel.at[0], rbuf.at[:, k, y, :, my_lanes], local.at[9])
    own_sel.start()
    for e, r, c, _ in plane:
        go(remote(sel.at[e], rbuf.at[:, k, y, :, my_lanes], s_s.at[e], s_r.at[slot], (r, c)))

    for d, p in z_peers:
        remote(acts, afull.at[p, y], a_s.at[d], a_r.at[p], mate).wait_recv()
        go(remote(afull.at[p, y], afull.at[p, y], ay_s.at[d], ay_r.at[p], mate))
    go(remote(nxt, nfull.at[z, y], ny_s.at[0], ny_r.at[z], mate))
    for d, p in z_peers:
        remote(nxt, nfull.at[p, y], n_s.at[d], n_r.at[p], mate).wait_recv()
        go(remote(nfull.at[p, y], nfull.at[p, y], ny_s.at[d], ny_r.at[p], mate))

    for i in (0, 2):
        loads[i].wait()
    for d, c in col_peers:
        remote(grads, gfull.at[pl.ds(pl.multiple_of(c * gtok, gtok), gtok)],
               g_s.at[d], g_r.at[c], (row, c)).wait_recv()

    for d in range(nz):
        zs = flip(z, d, nz) if d else z
        remote(acts, afull.at[zs, 1 - y], ay_s.at[0], ay_r.at[zs], mate).wait_recv()
        term = lax.dot_general(
            gfull[pl.ds(pl.multiple_of(zs * 2 * tok, 2 * tok), 2 * tok)],
            afull[zs].reshape(2 * tok, width),
            (((0,), (0,)), ((), ())), preferred_element_type=F32,
        )
        if d == 0:
            gacc[...] = term
        else:
            gacc[...] += term

    loads[6].wait()
    left = lbuf[left_index[0, 0]]
    half[...] = lax.dot_general(
        left, gacc[...].astype(BF16), (((0,), (0,)), ((), ())), preferred_element_type=F32
    ).astype(BF16)

    own_sel.wait()
    for e, r, c, s in plane:
        ys, qs = s // 4, s % 4
        src_lanes = pl.ds(pl.multiple_of((qs // 2) * lanes, 128), lanes)
        remote(sel.at[e], rbuf.at[:, qs % 2, ys, :, src_lanes], s_s.at[e], s_r.at[s],
               (r, c)).wait_recv()
    for i in (3, 4, 5):
        loads[i].wait()
    step = 256 if width % 256 == 0 else width
    right = as_matrix(rbuf[...])
    for n in range(0, width, step):
        cut = slice(n, n + step)
        rotated = jnp.dot(half[...], right[:, cut], preferred_element_type=F32)
        new_moment = 0.8 * mbuf[:, cut] + 0.2 * rotated
        new_second = 0.9 * sbuf[:, cut] + 0.1 * rotated * rotated
        scaled = (new_moment / (jnp.sqrt(new_second) + 1e-08)).astype(BF16)
        back[:, cut] = jnp.dot(left, scaled, preferred_element_type=F32).astype(BF16)

    loads[1].wait()
    for d in range(nz):
        zs = flip(z, d, nz) if d else z
        remote(nxt, nfull.at[zs, 1 - y], ny_s.at[0], ny_r.at[zs], mate).wait_recv()
    rows = nfull.shape[0] * nfull.shape[1] * nfull.shape[2]
    for n in range(0, width, step):
        cut = slice(n, n + step)
        full = lax.dot_general(
            back[...], right[cut, :], (((1,), (1,)), ((), ())), preferred_element_type=F32
        )
        ubuf[:, cut] = full.astype(BF16)
        new_weight = (wbuf[:, cut].astype(F32) - 0.001 * full).astype(BF16)
        term = lax.dot_general(
            nfull[:, :, :, cut].reshape(rows, step), new_weight,
            (((1,), (1,)), ((), ())), preferred_element_type=F32,
        )
        if n == 0:
            part[...] = term
        else:
            part[...] += term
    put = pltpu.make_async_copy(ubuf, update, local.at[3])
    put.start()

    share = rows // nc
    rsend[...] = part[...].astype(BF16).reshape(nc, share, part.shape[1])
    for d, c in col_peers:
        go(remote(rsend.at[c], rrecv.at[d - 1], r_s.at[d], r_r.at[d], (row, c)))
    total = part[pl.ds(pl.multiple_of(col * share, share), share)]
    for d, c in col_peers:
        remote(rsend.at[c], rrecv.at[d - 1], r_s.at[d], r_r.at[d], (row, c)).wait_recv()
        total = total + rrecv[d - 1].astype(F32)
    obuf[...] = total.astype(BF16)
    put_out = pltpu.make_async_copy(obuf, out, local.at[4])
    put_out.start()

    for copy in sends:
        copy.wait_send()

    @pl.when(z % 2 == k)
    def _():
        for copy in bank_sends:
            copy.wait_send()

    put.wait()
    put_out.wait()


def per_device(
    acts, grads, next_acts, weight, moment, second, left_bank, right_bank, left_index, right_index,
    *, nr, nc,
):
    nz = nr // 2
    tok, width = acts.shape
    gtok, bo = grads.shape
    ntok = next_acts.shape[0]
    bank, rrows, _ = right_bank.shape
    lanes = width // 2
    share = nr * ntok // nc
    dma = pltpu.SemaphoreType.DMA
    anyspace = pl.BlockSpec(memory_space=pl.ANY)
    smem = pl.BlockSpec(memory_space=pltpu.SMEM)
    return pl.pallas_call(
        functools.partial(kernel, nz, nc),
        out_shape=(
            jax.ShapeDtypeStruct(weight.shape, BF16),
            jax.ShapeDtypeStruct((share, bo), BF16),
        ),
        in_specs=[anyspace] * 8 + [smem] * 2,
        out_specs=(anyspace, anyspace),
        scratch_shapes=[
            pltpu.VMEM((nz, 2, tok, width), BF16),
            pltpu.VMEM((nc * gtok, bo), BF16),
            pltpu.VMEM((nz, 2, ntok, width), BF16),
            pltpu.VMEM(weight.shape, BF16),
            pltpu.VMEM(weight.shape, F32),
            pltpu.VMEM(weight.shape, F32),
            pltpu.VMEM(left_bank.shape, BF16),
            pltpu.VMEM((nz // 2, bank, rrows, lanes), BF16),
            pltpu.VMEM((8, nz // 2, rrows, lanes), BF16),
            pltpu.VMEM((nz // 2, 2, 2, rrows, width), BF16),
            pltpu.VMEM((8, 128), jnp.int32),
            pltpu.VMEM((8, 8, 128), jnp.int32),
            pltpu.SMEM((8, 8, 128), jnp.int32),
            pltpu.VMEM(weight.shape, F32),
            pltpu.VMEM(weight.shape, BF16),
            pltpu.VMEM(weight.shape, BF16),
            pltpu.VMEM((nr * ntok, bo), F32),
            pltpu.VMEM((nc, share, bo), BF16),
            pltpu.VMEM((nc - 1, share, bo), BF16),
            pltpu.VMEM(weight.shape, BF16),
            pltpu.VMEM((share, bo), BF16),
            dma((10,)),
            dma((nz,)), dma((nz,)), dma((nz,)), dma((nz,)),
            dma((nz,)), dma((nz,)), dma((nz,)), dma((nz,)),
            dma((nz,)), dma((nz // 2,)),
            dma((nc,)), dma((nc,)),
            dma((8,)), dma((8,)), dma((8,)), dma((8,)),
            dma((nc,)), dma((nc,)),
        ],
        compiler_params=pltpu.CompilerParams(
            collective_id=0, has_side_effects=True, vmem_limit_bytes=60 * 2**20,
        ),
    )(acts, grads, next_acts, weight, moment, second, left_bank, right_bank, left_index,
      right_index)


def solution(mesh):
    nr, nc = mesh.shape["row"], mesh.shape["col"]
    return jax.shard_map(
        functools.partial(per_device, nr=nr, nc=nc),
        mesh=mesh,
        in_specs=(
            P("row", "col"), P("col", "row"), P("row", "col"), P("row", "col"),
            P("row", "col"), P("row", "col"), P(), P(None, "row", None),
            P("row", "col"), P("row", "col"),
        ),
        out_specs=(P("row", "col"), P("col", "row")),
        check_vma=False,
    )
```

time: 141 us -> 67.9 us (0.48)
  blocking collectives: 82.6 us -> 0 us
  Pallas kernels: 0 us -> 63.3 us
  waiting for transfers between devices: 19.8 us -> 0 us
  between operations: 15.4 us -> 1.94 us
  matrix products: 10.9 us -> 0 us
  local copies, waits for them, and re-layouts: 7.28 us -> 2.55 us
  starting transfers between devices: 3.77 us -> 0 us
    all_gather x3 -> x0, blocking collectives: 82.6 us -> none  [the longest x1 60.7 us: per_device(): full_next = lax.all_gather(next_acts, 'row', axis=0, tiled=True)]
    pallas_call x0 -> x1, Pallas kernels: none -> 63.3 us  [per_device(): pl.pallas_call(functools.partial(kernel, nz, nc), out_shape=(jax.ShapeDty...]
    unnamed x3 -> x0, waiting for transfers between devices: 19.8 us -> none
    dot_general x4 -> x0, matrix products: 10.9 us -> none  [the longest x1 3.29 us: per_device(): rotated = jnp.dot(half, right_basis, preferred_element_type=f32)]
    all_to_all x1 -> x0, starting transfers between devices: 3.69 us -> none  [per_device(): lax.all_to_all(outgoing, 'row', split_axis=0, concat_axis=0, tiled=True)]
    unnamed x12 -> x4, local copies, waits for them, and re-layouts: 5.6 us -> 2.55 us
    gather x1 -> x0, local copies, waits for them, and re-layouts: 1.68 us -> none  [per_device(): outgoing = jnp.take(right_bank, all_picks, axis=0)]
  transfers between devices with their start and end apart: 3 -> 0, of which waited for: 1 -> 0; matrix products, arithmetic and copies ran while one was open for 6% -> 0% of each run, Pallas kernels for 0% -> 0%
where the time goes in v1:
time: 67.9 us; the launch traced here: 67.8 us
  Pallas kernels  63.3 us (93%)
  local copies, waits for them, and re-layouts  2.55 us (4%)
  between operations  1.94 us (3%)
    pallas_call x1, Pallas kernels, per_device(): pl.pallas_call(functools.partial(kernel, nz, nc), out_shape=(jax.ShapeDty...  63.3 us
    unnamed x4, local copies, waits for them, and re-layouts  2.55 us

profile of v1, /device:TPU:0, one launch (start us, length us, event | category | flops | bytes accessed | tf_op | source)
XLA Modules:
  0.0 67.8 jit_solution(4565984924156886410)
XLA Ops:
  1.9 63.3 %shard_map.113 = (bf16[384,768]{1,0:T(8,128)(2,1)}, bf16[64,384]{1,0:T(8,128)(2,1)}) custom-call(bf16[128,768]{1,0:T(8,128)(2,1)} %acts.1, bf16[256,384]{1,0:T(8,128)(2,1)} %grads.1, bf16[32,768]{1,0:T(8,128)(2,1)} %nxt.1, bf16[384,768]{1,0:T(8,128)(2,1)} %weight.1, f32[384,768]{1,0:T(8,128)} %moment.1, f32[384,768]{1,0:T(8,128)} %second.1, ...), custom_call_target="tpu_custom_call" | custom-call | tf_op jit(solution)/shard_map/pallas_call | solution.py:260
  65.2 0.0 copy-start
  65.2 1.9 %copy.16 = bf16[384,768]{1,0:T(8,128)(2,1)} copy(bf16[384,768]{1,0:T(8,128)(2,1)} %get-tuple-element.4) | data formatting | bytes 1179648
  67.2 0.0 copy-done
  67.2 0.6 copy.17
Async XLA Ops:
  65.2 1.9 %copy-start = (bf16[64,384]{1,0:T(8,128)(2,1)S(1)}, bf16[64,384]{1,0:T(8,128)(2,1)}, u32[]{:S(2)}) copy-start(bf16[64,384]{1,0:T(8,128)(2,1)} %get-tuple-element.5) | copy-start | bytes 147460

commit v2 on v1

--- a/solution.py
+++ b/solution.py
@@ -91,7 +91,7 @@
         pl.semaphore_signal(barrier, inc=1, device_id=friend, device_id_type=MESH)
     pl.semaphore_wait(barrier, len(friends))
 
-    sends = []
+    sends, guards = [], []
 
     def go(copy):
         copy.start()
@@ -99,25 +99,35 @@
 
     for e, r, c, _ in plane:
         go(remote(my_pick, picks.at[slot], p_s.at[e], p_r.at[slot], (r, c)))
-    bank_sends = [
-        remote(right_bank.at[:, :, my_lanes], bz.at[z // 2], b_s.at[d], b_r.at[z // 2],
-               (2 * p + y, col))
-        for d, p in z_peers
-    ]
-
-    @pl.when(z % 2 == k)
-    def _():
-        for copy in bank_sends:
+    bank_src = right_bank.at[:, :, my_lanes]
+    up, down = (2 * (z + 1) + y, col), (2 * (z - 1) + y, col)
+    has_up, has_down = z < nz - 1, z > 0
+
+    def guarded(cond, copy):
+        @pl.when(cond)
+        def _():
             copy.start()
 
-    go(remote(acts, afull.at[z, y], ay_s.at[0], ay_r.at[z], mate))
-    for d, p in z_peers:
-        go(remote(acts, afull.at[z, y], a_s.at[d], a_r.at[z], (2 * p + y, col)))
+        guards.append((cond, copy))
+
+    def bank_copy(src, zs, ss, device):
+        return remote(src, bz.at[zs // 2], ss, b_r.at[zs // 2], device)
+
+    def both_ways(make, mine):
+        guarded(has_up & mine, make(0, up))
+        guarded(has_down & mine, make(1, down))
+
+    yes = z >= 0
+    go(remote(nxt, nfull.at[z, y], ny_s.at[0], ny_r.at[0], mate))
+    both_ways(lambda i, to: bank_copy(bank_src, z, b_s.at[nz + i], to), z % 2 == k)
+    both_ways(lambda i, to: remote(acts, afull.at[z, y], a_s.at[nz + i], a_r.at[z], to), yes)
+    go(remote(acts, afull.at[z, y], ay_s.at[z], ay_r.at[z], mate))
     for d, c in col_peers:
         go(remote(grads, gfull.at[pl.ds(pl.multiple_of(col * gtok, gtok), gtok)],
                   g_s.at[d], g_r.at[col], (row, c)))
-    for d, p in z_peers:
-        go(remote(nxt, nfull.at[z, y], n_s.at[d], n_r.at[z], (2 * p + y, col)))
+    loads[1].wait()
+    remote(nxt, nfull.at[z, 1 - y], ny_s.at[0], ny_r.at[0], mate).wait_recv()
+    both_ways(lambda i, to: remote(nfull.at[z], nfull.at[z], n_s.at[nz + i], n_r.at[z], to), yes)
 
     picks[slot] = my_pick[...]
     for e, r, c, s in plane:
@@ -126,17 +136,37 @@
     to_smem.start()
     to_smem.wait()
 
-    for d in range(nz):
-        zs = flip(z, d, nz) if d else z
-
-        @pl.when(zs % 2 == k)
-        def _(d=d, zs=zs):
-            if d == 0:
-                own_bank.wait()
+    @pl.when(z % 2 == k)
+    def _():
+        own_bank.wait()
+
+    def take(valid, copy):
+        @pl.when(valid)
+        def _():
+            copy.wait_recv()
+
+    def forward(hop, what):
+        for zs, valid, on, to in ((z - hop, z >= hop, has_up, up),
+                                  (z + hop, z + hop < nz, has_down, down)):
+            zs = lax.rem(zs + nz, nz)
+            if what == "bank":
+                valid = valid & (zs % 2 == k)
+                copy = bank_copy(bz.at[zs // 2], zs, b_s.at[zs], to)
+            elif what == "acts":
+                copy = remote(afull.at[zs, y], afull.at[zs, y], a_s.at[zs], a_r.at[zs], to)
             else:
-                remote(right_bank.at[:, :, my_lanes], bz.at[zs // 2], b_s.at[d],
-                       b_r.at[zs // 2], (2 * zs + y, col)).wait_recv()
-
+                copy = remote(nfull.at[zs], nfull.at[zs], n_s.at[zs], n_r.at[zs], to)
+            take(valid, copy)
+            if hop < nz - 1:
+                guarded(valid & on, copy)
+            if what == "acts":
+                guarded(valid, remote(afull.at[zs, y], afull.at[zs, y], ay_s.at[zs],
+                                      ay_r.at[zs], mate))
+
+    for hop in range(1, nz):
+        forward(hop, "bank")
+        if hop < nz - 1:
+            forward(hop, "acts")
     sel[0] = bz[:, picks_smem[slot, 0, 0]]
     for e, r, c, s in plane:
         sel[e] = bz[:, picks_smem[s, 0, 0]]
@@ -145,13 +175,10 @@
     for e, r, c, _ in plane:
         go(remote(sel.at[e], rbuf.at[:, k, y, :, my_lanes], s_s.at[e], s_r.at[slot], (r, c)))
 
-    for d, p in z_peers:
-        remote(acts, afull.at[p, y], a_s.at[d], a_r.at[p], mate).wait_recv()
-        go(remote(afull.at[p, y], afull.at[p, y], ay_s.at[d], ay_r.at[p], mate))
-    go(remote(nxt, nfull.at[z, y], ny_s.at[0], ny_r.at[z], mate))
-    for d, p in z_peers:
-        remote(nxt, nfull.at[p, y], n_s.at[d], n_r.at[p], mate).wait_recv()
-        go(remote(nfull.at[p, y], nfull.at[p, y], ny_s.at[d], ny_r.at[p], mate))
+
+    forward(nz - 1, "acts")
+    for hop in range(1, nz):
+        forward(hop, "next")
 
     for i in (0, 2):
         loads[i].wait()
@@ -196,10 +223,6 @@
         scaled = (new_moment / (jnp.sqrt(new_second) + 1e-08)).astype(BF16)
         back[:, cut] = jnp.dot(left, scaled, preferred_element_type=F32).astype(BF16)
 
-    loads[1].wait()
-    for d in range(nz):
-        zs = flip(z, d, nz) if d else z
-        remote(nxt, nfull.at[zs, 1 - y], ny_s.at[0], ny_r.at[zs], mate).wait_recv()
     rows = nfull.shape[0] * nfull.shape[1] * nfull.shape[2]
     for n in range(0, width, step):
         cut = slice(n, n + step)
@@ -234,9 +257,9 @@
     for copy in sends:
         copy.wait_send()
 
-    @pl.when(z % 2 == k)
-    def _():
-        for copy in bank_sends:
+    for cond, copy in guards:
+        @pl.when(cond)
+        def _(copy=copy):
             copy.wait_send()
 
     put.wait()
@@ -288,9 +311,9 @@
             pltpu.VMEM(weight.shape, BF16),
             pltpu.VMEM((share, bo), BF16),
             dma((10,)),
-            dma((nz,)), dma((nz,)), dma((nz,)), dma((nz,)),
-            dma((nz,)), dma((nz,)), dma((nz,)), dma((nz,)),
-            dma((nz,)), dma((nz // 2,)),
+            dma((nz + 2,)), dma((nz,)), dma((nz,)), dma((nz,)),
+            dma((nz + 2,)), dma((nz,)), dma((1,)), dma((1,)),
+            dma((nz + 2,)), dma((nz // 2,)),
             dma((nc,)), dma((nc,)),
             dma((8,)), dma((8,)), dma((8,)), dma((8,)),
             dma((nc,)), dma((nc,)),

time: 67.9 us -> 60.6 us (0.89)
  Pallas kernels: 63.3 us -> 55.9 us
    pallas_call x1, Pallas kernels: 63.3 us -> 55.9 us  [per_device(): pl.pallas_call(functools.partial(kernel, nz, nc), out_shape=(jax.ShapeDty...]
where the time goes in v2:
time: 60.6 us; the launch traced here: 60.4 us
  Pallas kernels  55.9 us (92%)
  local copies, waits for them, and re-layouts  2.55 us (4%)
  between operations  1.94 us (3%)
    pallas_call x1, Pallas kernels, per_device(): pl.pallas_call(functools.partial(kernel, nz, nc), out_shape=(jax.ShapeDty...  55.9 us
    unnamed x4, local copies, waits for them, and re-layouts  2.55 us

profile of v2, /device:TPU:0, one launch (start us, length us, event | category | flops | bytes accessed | tf_op | source)
XLA Modules:
  0.0 60.4 jit_solution(3430443389954269312)
XLA Ops:
  1.9 55.9 %shard_map.113 = (bf16[384,768]{1,0:T(8,128)(2,1)}, bf16[64,384]{1,0:T(8,128)(2,1)}) custom-call(bf16[128,768]{1,0:T(8,128)(2,1)} %acts.1, bf16[256,384]{1,0:T(8,128)(2,1)} %grads.1, bf16[32,768]{1,0:T(8,128)(2,1)} %nxt.1, bf16[384,768]{1,0:T(8,128)(2,1)} %weight.1, f32[384,768]{1,0:T(8,128)} %moment.1, f32[384,768]{1,0:T(8,128)} %second.1, ...), custom_call_target="tpu_custom_call" | custom-call | tf_op jit(solution)/shard_map/pallas_call | solution.py:283
  57.8 0.0 copy-start
  57.8 1.9 %copy.16 = bf16[384,768]{1,0:T(8,128)(2,1)} copy(bf16[384,768]{1,0:T(8,128)(2,1)} %get-tuple-element.4) | data formatting | bytes 1179648
  59.8 0.0 copy-done
  59.8 0.6 %copy.17 = bf16[64,384]{1,0:T(8,128)(2,1)} copy(bf16[64,384]{1,0:T(8,128)(2,1)S(1)} %copy-done) | data formatting | bytes 98304
Async XLA Ops:
  57.8 1.9 %copy-start = (bf16[64,384]{1,0:T(8,128)(2,1)S(1)}, bf16[64,384]{1,0:T(8,128)(2,1)}, u32[]{:S(2)}) copy-start(bf16[64,384]{1,0:T(8,128)(2,1)} %get-tuple-element.5) | copy-start | bytes 147460

commit v3 on v2

--- a/solution.py
+++ b/solution.py
@@ -35,7 +35,7 @@
     afull, gfull, nfull, wbuf, mbuf, sbuf, lbuf, bz, sel, rbuf,
     my_pick, picks, picks_smem, gacc, half, back, part, rsend, rrecv, ubuf, obuf,
     local, a_s, a_r, ay_s, ay_r, n_s, n_r, ny_s, ny_r, b_s, b_r,
-    g_s, g_r, p_s, p_r, s_s, s_r, r_s, r_r,
+    g_s, g_r, p_s, p_r, s_s, s_r, own_s, r_s, r_r,
 ):
     row, col = lax.axis_index("row"), lax.axis_index("col")
     z, y = row // 2, row % 2
@@ -91,7 +91,7 @@
         pl.semaphore_signal(barrier, inc=1, device_id=friend, device_id_type=MESH)
     pl.semaphore_wait(barrier, len(friends))
 
-    sends, guards = [], []
+    sends, guards, handed = [], [], []
 
     def go(copy):
         copy.start()
@@ -136,9 +136,38 @@
     to_smem.start()
     to_smem.wait()
 
+    def place(zs, slot_from):
+        ys, qs = slot_from // 4, slot_from % 4
+        at = pl.ds(pl.multiple_of((qs // 2) * lanes, 128), lanes)
+        return rbuf.at[zs // 2, qs % 2, ys, :, at]
+
+    def plane_copy(zs, e, s, device):
+        i = zs // 2
+        return remote(sel.at[i, e], place(zs, s), s_s.at[i, e], s_r.at[i, s], device)
+
+    def own_copy(zs):
+        return pltpu.make_async_copy(sel.at[zs // 2, 0], place(zs, slot), own_s.at[zs // 2])
+
+    def hand_out(zs, valid):
+        @pl.when(valid)
+        def _():
+            for e, s in [(0, slot)] + [(e, s) for e, _, _, s in plane]:
+                pick = picks_smem[s, 0, 0]
+                piece = bz[zs // 2, 0]
+                for b in range(1, bz.shape[1]):
+                    piece = jnp.where(pick == b, bz[zs // 2, b], piece)
+                sel[zs // 2, e] = piece
+            own_copy(zs).start()
+            for e, r, c, _ in plane:
+                plane_copy(zs, e, slot, (r, c)).start()
+
+        handed.append((zs, valid))
+
     @pl.when(z % 2 == k)
     def _():
         own_bank.wait()
+
+    hand_out(z, z % 2 == k)
 
     def take(valid, copy):
         @pl.when(valid)
@@ -159,6 +188,8 @@
             take(valid, copy)
             if hop < nz - 1:
                 guarded(valid & on, copy)
+            if what == "bank":
+                hand_out(zs, valid)
             if what == "acts":
                 guarded(valid, remote(afull.at[zs, y], afull.at[zs, y], ay_s.at[zs],
                                       ay_r.at[zs], mate))
@@ -167,15 +198,6 @@
         forward(hop, "bank")
         if hop < nz - 1:
             forward(hop, "acts")
-    sel[0] = bz[:, picks_smem[slot, 0, 0]]
-    for e, r, c, s in plane:
-        sel[e] = bz[:, picks_smem[s, 0, 0]]
-    own_sel = pltpu.make_async_copy(sel.at[0], rbuf.at[:, k, y, :, my_lanes], local.at[9])
-    own_sel.start()
-    for e, r, c, _ in plane:
-        go(remote(sel.at[e], rbuf.at[:, k, y, :, my_lanes], s_s.at[e], s_r.at[slot], (r, c)))
-
-
     forward(nz - 1, "acts")
     for hop in range(1, nz):
         forward(hop, "next")
@@ -205,12 +227,14 @@
         left, gacc[...].astype(BF16), (((0,), (0,)), ((), ())), preferred_element_type=F32
     ).astype(BF16)
 
-    own_sel.wait()
-    for e, r, c, s in plane:
-        ys, qs = s // 4, s % 4
-        src_lanes = pl.ds(pl.multiple_of((qs // 2) * lanes, 128), lanes)
-        remote(sel.at[e], rbuf.at[:, qs % 2, ys, :, src_lanes], s_s.at[e], s_r.at[s],
-               (r, c)).wait_recv()
+    for i in range(nz // 2):
+        for e, r, c, s in plane:
+            plane_copy(2 * i, e, s, (r, c)).wait_recv()
+    for zs, valid in handed:
+        @pl.when(valid)
+        def _(zs=zs):
+            own_copy(zs).wait()
+
     for i in (3, 4, 5):
         loads[i].wait()
     step = 256 if width % 256 == 0 else width
@@ -261,6 +285,12 @@
         @pl.when(cond)
         def _(copy=copy):
             copy.wait_send()
+
+    for zs, valid in handed:
+        @pl.when(valid)
+        def _(zs=zs):
+            for e, r, c, _ in plane:
+                plane_copy(zs, e, slot, (r, c)).wait_send()
 
     put.wait()
     put_out.wait()
@@ -297,7 +327,7 @@
             pltpu.VMEM(weight.shape, F32),
             pltpu.VMEM(left_bank.shape, BF16),
             pltpu.VMEM((nz // 2, bank, rrows, lanes), BF16),
-            pltpu.VMEM((8, nz // 2, rrows, lanes), BF16),
+            pltpu.VMEM((nz // 2, 8, rrows, lanes), BF16),
             pltpu.VMEM((nz // 2, 2, 2, rrows, width), BF16),
             pltpu.VMEM((8, 128), jnp.int32),
             pltpu.VMEM((8, 8, 128), jnp.int32),
@@ -315,7 +345,7 @@
             dma((nz + 2,)), dma((nz,)), dma((1,)), dma((1,)),
             dma((nz + 2,)), dma((nz // 2,)),
             dma((nc,)), dma((nc,)),
-            dma((8,)), dma((8,)), dma((8,)), dma((8,)),
+            dma((8,)), dma((8,)), dma((nz // 2, 8)), dma((nz // 2, 8)), dma((nz // 2,)),
             dma((nc,)), dma((nc,)),
         ],
         compiler_params=pltpu.CompilerParams(

time: 60.6 us -> 53 us (0.87)
  Pallas kernels: 55.9 us -> 48.3 us
    pallas_call x1, Pallas kernels: 55.9 us -> 48.3 us  [per_device(): pl.pallas_call(functools.partial(kernel, nz, nc), out_shape=(jax.ShapeDty...]
where the time goes in v3:
time: 53 us; the launch traced here: 52.8 us
  Pallas kernels  48.3 us (91%)
  local copies, waits for them, and re-layouts  2.55 us (5%)
  between operations  1.94 us (4%)
    pallas_call x1, Pallas kernels, per_device(): pl.pallas_call(functools.partial(kernel, nz, nc), out_shape=(jax.ShapeDty...  48.3 us
    unnamed x4, local copies, waits for them, and re-layouts  2.55 us

profile of v3, /device:TPU:0, one launch (start us, length us, event | category | flops | bytes accessed | tf_op | source)
XLA Modules:
  0.0 52.8 jit_solution(13114895348089012676)
XLA Ops:
  1.9 48.3 %shard_map.113 = (bf16[384,768]{1,0:T(8,128)(2,1)}, bf16[64,384]{1,0:T(8,128)(2,1)}) custom-call(bf16[128,768]{1,0:T(8,128)(2,1)} %acts.1, bf16[256,384]{1,0:T(8,128)(2,1)} %grads.1, bf16[32,768]{1,0:T(8,128)(2,1)} %nxt.1, bf16[384,768]{1,0:T(8,128)(2,1)} %weight.1, f32[384,768]{1,0:T(8,128)} %moment.1, f32[384,768]{1,0:T(8,128)} %second.1, ...), custom_call_target="tpu_custom_call" | custom-call | tf_op jit(solution)/shard_map/pallas_call | solution.py:313
  50.2 0.0 copy-start
  50.2 1.9 %copy.16 = bf16[384,768]{1,0:T(8,128)(2,1)} copy(bf16[384,768]{1,0:T(8,128)(2,1)} %get-tuple-element.4) | data formatting | bytes 1179648
  52.2 0.0 copy-done
  52.2 0.6 %copy.17 = bf16[64,384]{1,0:T(8,128)(2,1)} copy(bf16[64,384]{1,0:T(8,128)(2,1)S(1)} %copy-done) | data formatting | bytes 98304
Async XLA Ops:
  50.2 1.9 %copy-start = (bf16[64,384]{1,0:T(8,128)(2,1)S(1)}, bf16[64,384]{1,0:T(8,128)(2,1)}, u32[]{:S(2)}) copy-start(bf16[64,384]{1,0:T(8,128)(2,1)} %get-tuple-element.5) | copy-start | bytes 147460

commit v4 on v3

--- a/solution.py
+++ b/solution.py
@@ -254,22 +254,22 @@
             back[...], right[cut, :], (((1,), (1,)), ((), ())), preferred_element_type=F32
         )
         ubuf[:, cut] = full.astype(BF16)
-        new_weight = (wbuf[:, cut].astype(F32) - 0.001 * full).astype(BF16)
+        half[:, cut] = (wbuf[:, cut].astype(F32) - 0.001 * full).astype(BF16)
+    put = pltpu.make_async_copy(ubuf, update, local.at[3])
+    put.start()
+
+    share = rows // nc
+    hz, hc, side = nz // 2, nc // 2, col // (nc // 2)
+    for turn, at in enumerate((1 - side, side)):
         term = lax.dot_general(
-            nfull[:, :, :, cut].reshape(rows, step), new_weight,
+            nfull[pl.ds(at * hz, hz)].reshape(rows // 2, width), half[...],
             (((1,), (1,)), ((), ())), preferred_element_type=F32,
         )
-        if n == 0:
-            part[...] = term
-        else:
-            part[...] += term
-    put = pltpu.make_async_copy(ubuf, update, local.at[3])
-    put.start()
-
-    share = rows // nc
-    rsend[...] = part[...].astype(BF16).reshape(nc, share, part.shape[1])
-    for d, c in col_peers:
-        go(remote(rsend.at[c], rrecv.at[d - 1], r_s.at[d], r_r.at[d], (row, c)))
+        part[pl.ds(pl.multiple_of(at * (rows // 2), rows // 2), rows // 2)] = term
+        rsend[pl.ds(at * hc, hc)] = term.astype(BF16).reshape(hc, share, part.shape[1])
+        for d, c in col_peers:
+            if (d >= hc) == (turn == 0):
+                go(remote(rsend.at[c], rrecv.at[d - 1], r_s.at[d], r_r.at[d], (row, c)))
     total = part[pl.ds(pl.multiple_of(col * share, share), share)]
     for d, c in col_peers:
         remote(rsend.at[c], rrecv.at[d - 1], r_s.at[d], r_r.at[d], (row, c)).wait_recv()
@@ -294,6 +294,24 @@
 
     put.wait()
     put_out.wait()
+
+
+def finish(update_in, out_in, update, out, ubuf, obuf, sems):
+    rows = ubuf.shape[0] // 4
+    gets, puts = [], []
+    for i in range(4):
+        cut = pl.ds(i * rows, rows)
+        gets.append(pltpu.make_async_copy(update_in.at[cut], ubuf.at[cut], sems.at[i]))
+        puts.append(pltpu.make_async_copy(ubuf.at[cut], update.at[cut], sems.at[5 + i]))
+    gets.append(pltpu.make_async_copy(out_in, obuf, sems.at[4]))
+    puts.append(pltpu.make_async_copy(obuf, out, sems.at[9]))
+    for get in gets:
+        get.start()
+    for get, put in zip(gets, puts):
+        get.wait()
+        put.start()
+    for put in puts:
+        put.wait()
 
 
 def per_device(
@@ -310,7 +328,7 @@
     dma = pltpu.SemaphoreType.DMA
     anyspace = pl.BlockSpec(memory_space=pl.ANY)
     smem = pl.BlockSpec(memory_space=pltpu.SMEM)
-    return pl.pallas_call(
+    update, out = pl.pallas_call(
         functools.partial(kernel, nz, nc),
         out_shape=(
             jax.ShapeDtypeStruct(weight.shape, BF16),
@@ -353,6 +371,18 @@
         ),
     )(acts, grads, next_acts, weight, moment, second, left_bank, right_bank, left_index,
       right_index)
+    return pl.pallas_call(
+        finish,
+        out_shape=(
+            jax.ShapeDtypeStruct(weight.shape, BF16),
+            jax.ShapeDtypeStruct((share, bo), BF16),
+        ),
+        in_specs=[anyspace] * 2,
+        out_specs=(anyspace, anyspace),
+        scratch_shapes=[
+            pltpu.VMEM(weight.shape, BF16), pltpu.VMEM((share, bo), BF16), dma((10,)),
+        ],
+    )(update, out)
 
 
 def solution(mesh):

time: 53 us -> 51.9 us (0.979)
  local copies, waits for them, and re-layouts: 2.55 us -> 0 us
  Pallas kernels: 48.3 us -> 49.8 us
    unnamed x4 -> x0, local copies, waits for them, and re-layouts: 2.55 us -> none
    pallas_call x0 -> x1, Pallas kernels: none -> 1.88 us  [per_device(): pl.pallas_call(finish, out_shape=(jax.ShapeDtypeStruct(weight.shape, BF16...]
where the time goes in v4:
time: 51.9 us; the launch traced here: 51.8 us
  Pallas kernels  49.8 us (96%)
  between operations  1.93 us (4%)
    pallas_call x1, Pallas kernels, per_device(): pl.pallas_call(functools.partial(kernel, nz, nc), out_shape=(jax.ShapeDty...  48 us
    pallas_call x1, Pallas kernels, per_device(): pl.pallas_call(finish, out_shape=(jax.ShapeDtypeStruct(weight.shape, BF16...  1.88 us

profile of v4, /device:TPU:0, one launch (start us, length us, event | category | flops | bytes accessed | tf_op | source)
XLA Modules:
  0.0 51.8 jit_solution(10407587577314579398)
XLA Ops:
  1.9 48.0 %shard_map.113 = (bf16[384,768]{1,0:T(8,128)(2,1)}, bf16[64,384]{1,0:T(8,128)(2,1)}) custom-call(bf16[128,768]{1,0:T(8,128)(2,1)} %acts.1, bf16[256,384]{1,0:T(8,128)(2,1)} %grads.1, bf16[32,768]{1,0:T(8,128)(2,1)} %nxt.1, bf16[384,768]{1,0:T(8,128)(2,1)} %weight.1, f32[384,768]{1,0:T(8,128)} %moment.1, f32[384,768]{1,0:T(8,128)} %second.1, ...), custom_call_target="tpu_custom_call" | custom-call | tf_op jit(solution)/shard_map/pallas_call | solution.py:331
  49.9 1.9 %shard_map.114 = (bf16[384,768]{1,0:T(8,128)(2,1)}, bf16[64,384]{1,0:T(8,128)(2,1)}) custom-call(bf16[384,768]{1,0:T(8,128)(2,1)} %get-tuple-element.4.update_in, bf16[64,384]{1,0:T(8,128)(2,1)} %get-tuple-element.5.out_in), custom_call_target="tpu_custom_call" | custom-call | tf_op jit(solution)/shard_map/pallas_call | solution.py:374
